TPU v7x, 256 devices: a whole 4x4x8 slice. The times are simulated.
256 devices in a mesh: panel: 16 (over y_hi, z), dir: 8 (over x, core), freq: 2 (over y_lo).
Axes of the slice: x: 4, y: 4 (y_hi: 2, y_lo: 2; y = y_hi * 2 + y_lo), z: 8, core: 2. Of those that a mesh axis runs over, the one named last changes fastest.
Arguments:
- sources: bfloat16 [4, 2, 64, 65536], P('freq', None, None, 'panel'), may hold values from -0.046875 to 0.046875
- panel_geom: float32 [4, 65536], P(None, 'panel'), may hold values from -150 to 150, as said below
- drift_cot: float32 [4, 64], P('freq'), may hold values from -4 to 4
- freq_index: int32 [4], P('freq'), may hold values from 0 to 511
- heading_dir: int32 [64], replicated, may hold values from 0 to 4095
Outputs:
- source_grad: float32 [4, 2, 64, 65536], P('freq', None, None, ('panel', 'dir'))
- geom_grad: float32 [4, 65536], P(None, ('panel', 'dir'))
Inputs may be any that keep to these rules, and one draw needn't show every extreme that they name: `panel_geom`: rows are panel centre x, y, z in metres, z at or below the water line, and panel area from 0.5 to 2.
All inputs are finite; a program needn't handle non-finite values.
Results may differ from a plain program's by a relative error of at most 0.00042.
Values may be sent and summed in bfloat16 or wider, within the bound.
A program may use at most 64 MiB of HBM per device.

v0:
```python
import math
import jax
import jax.numpy as jnp
from jax import lax
from jax.sharding import PartitionSpec as P

ND = 4096
FREQS = 512
gravity = 9.81
omega_low = 0.6
omega_span = 0.8
drift_gain = 5.0
cross_gain = 0.5
shape_scale = 100.0


def wave_numbers(freq_index):
    omega = omega_low + omega_span * freq_index.astype(jnp.float32) / FREQS
    return omega * omega / gravity


def direction_angles(dir_ids):
    return dir_ids.astype(jnp.float32) * (2.0 * math.pi / ND)


def phase_terms(geometry, wave, angles):
    amplitude = geometry[3] * jnp.exp(wave * geometry[2])
    phase = wave * (
        geometry[0][:, None] * jnp.cos(angles)[None, :]
        + geometry[1][:, None] * jnp.sin(angles)[None, :]
    )
    return (amplitude[:, None] * jnp.cos(phase), -amplitude[:, None] * jnp.sin(phase))


def kochin_block(sig, geometry, wave, dir_ids):
    heads = sig.shape[1]
    real, imag = phase_terms(geometry, wave, direction_angles(dir_ids))
    width = real.shape[1]
    phases = jnp.concatenate([real, imag], 1).astype(jnp.bfloat16)
    prod = jnp.dot(sig.reshape(2 * heads, sig.shape[2]), phases, preferred_element_type=jnp.float32)
    kreal = prod[:heads, :width] - prod[heads:, width:]
    kimag = prod[:heads, width:] + prod[heads:, :width]
    return jnp.stack([kreal, kimag])


def cotangent(kochin, wave, dir_ids, weight, heading_dir):
    angles = direction_angles(dir_ids)
    slope = -drift_gain * wave / math.sqrt(ND)
    beta = direction_angles(heading_dir)
    hit = (dir_ids[None, :] == heading_dir[:, None]).astype(jnp.float32)
    along = 2.0 * slope * jnp.cos(angles)[None, :]
    real_part = weight[:, None] * (along * kochin[0] - cross_gain * jnp.cos(beta)[:, None] * hit)
    imag_part = weight[:, None] * (along * kochin[1])
    return jnp.stack([real_part, imag_part]).astype(jnp.bfloat16)


def backward_block(sig, geometry, wave, dir_ids, cot):
    heads = sig.shape[1]
    angles = direction_angles(dir_ids)
    real, imag = phase_terms(geometry, wave, angles)
    width = real.shape[1]
    phases = jnp.concatenate([real, imag], 1).astype(jnp.bfloat16)
    mixed = jnp.concatenate(
        [jnp.concatenate([cot[0], cot[1]], 1), jnp.concatenate([cot[1], -cot[0]], 1)], 0
    )
    flat = sig.reshape(2 * heads, sig.shape[2])
    dsig = jnp.dot(mixed, phases.T, preferred_element_type=jnp.float32)
    dphase = jnp.dot(flat.T, mixed, preferred_element_type=jnp.float32)
    d_real = dphase[:, :width]
    d_imag = dphase[:, width:]
    twist = d_real * imag - d_imag * real
    swell = d_real * real + d_imag * imag
    shape = jnp.stack(
        [
            wave * jnp.sum(twist * jnp.cos(angles)[None, :], 1),
            wave * jnp.sum(twist * jnp.sin(angles)[None, :], 1),
            wave * jnp.sum(swell, 1),
            jnp.sum(swell, 1) / geometry[3],
        ]
    )
    return (dsig, shape)


def body(sources, panel_geom, drift_cot, freq_index, heading_dir):
    local_freqs = sources.shape[0]
    heads = sources.shape[2]
    panels = sources.shape[3]
    dir_count = ND // lax.axis_size("dir")
    dir_ids = lax.axis_index("dir") * dir_count + jnp.arange(dir_count, dtype=jnp.int32)
    waves = wave_numbers(freq_index)
    block = min(panels, 512)
    steps = panels // block
    kochin_parts = []
    for freq in range(local_freqs):

        def add_block(step, total):
            start = step * block
            sig = lax.dynamic_slice_in_dim(sources[freq], start, block, 2)
            geometry = lax.dynamic_slice_in_dim(panel_geom, start, block, 1)
            return total + kochin_block(sig, geometry, waves[freq], dir_ids)

        kochin_parts.append(
            lax.fori_loop(0, steps, add_block, jnp.zeros((2, heads, dir_count), jnp.float32))
        )
    partial_kochin = jnp.stack(kochin_parts)
    kochin = lax.psum(partial_kochin, "panel")
    cot = jnp.stack(
        [
            cotangent(kochin[freq], waves[freq], dir_ids, drift_cot[freq], heading_dir)
            for freq in range(local_freqs)
        ]
    )
    grads = []
    shape_total = jnp.zeros((4, panels), jnp.float32)
    for freq in range(local_freqs):

        def back_block(step, carry):
            grads_acc, shape_acc = carry
            start = step * block
            sig = lax.dynamic_slice_in_dim(sources[freq], start, block, 2)
            geometry = lax.dynamic_slice_in_dim(panel_geom, start, block, 1)
            dsig, shape = backward_block(sig, geometry, waves[freq], dir_ids, cot[freq])
            grads_acc = lax.dynamic_update_slice_in_dim(grads_acc, dsig, start, 1)
            old_shape = lax.dynamic_slice_in_dim(shape_acc, start, block, 1)
            shape_acc = lax.dynamic_update_slice_in_dim(shape_acc, old_shape + shape, start, 1)
            return (grads_acc, shape_acc)

        grads_freq, shape_total = lax.fori_loop(
            0, steps, back_block, (jnp.zeros((2 * heads, panels), jnp.float32), shape_total)
        )
        grads.append(grads_freq)
    grads_all = jnp.stack(grads).reshape(local_freqs, 2, heads, panels)
    source_part, shape_part = (
        lax.psum_scatter(grads_all, "dir", scatter_dimension=3, tiled=True),
        lax.psum_scatter(shape_total, "dir", scatter_dimension=1, tiled=True),
    )
    shape_all = lax.psum(shape_part, "freq")
    return (source_part, shape_scale * shape_all)


def solution(mesh):
    return jax.shard_map(
        body,
        mesh=mesh,
        in_specs=(
            P("freq", None, None, "panel"),
            P(None, "panel"),
            P("freq", None),
            P("freq"),
            P(),
        ),
        out_specs=(P("freq", None, None, ("panel", "dir")), P(None, ("panel", "dir"))),
        check_vma=False,
    )
```

profile of v0, /device:TPU:8, one launch (start us, length us, event | category | flops | bytes accessed | tf_op | source)
XLA Modules:
  0.0 536.5 jit_solution(602441275165219904)
XLA Ops:
  7.9 70.9 %while.75 = (s32[]{:T(128)}, f32[2,64,512]{2,1,0:T(8,128)S(1)}, bf16[2,2,64,4096]{3,2,1,0:T(8,128)(2,1)}, f32[4,4096]{1,0:T(4,128)}, f32[2]{0:T(128)S(1)}, /*ind...) while((s32[]{:T(128)}, f32[2,64,512]{2,1,0:T(8,128)S(1)}, ...), condition=%wide.region_3.0_spmd.clone, body=%wide.region_2.0_spmd.clone.sunk | while | flops 138677248 | bytes 6719753 | solution.py:103
  8.6 1.5 constant_dynamic-slice_fusion.23
  10.1 4.9 multiply_convert_fusion.7
  15.0 1.3 slice.600
  17.4 1.5 constant_dynamic-slice_fusion.23
  18.9 4.9 multiply_convert_fusion.7
  23.8 1.3 slice.600
  26.3 1.5 constant_dynamic-slice_fusion.23
  27.8 4.9 multiply_convert_fusion.7
  32.7 1.3 slice.600
  35.2 1.5 constant_dynamic-slice_fusion.23
  36.7 4.9 multiply_convert_fusion.7
  41.6 1.3 slice.600
  44.0 1.5 constant_dynamic-slice_fusion.23
  45.5 4.9 multiply_convert_fusion.7
  50.4 1.3 slice.600
  52.9 1.5 constant_dynamic-slice_fusion.23
  54.4 4.9 multiply_convert_fusion.7
  59.3 1.3 slice.600
  61.8 1.5 constant_dynamic-slice_fusion.23
  63.3 4.9 multiply_convert_fusion.7
  68.2 1.3 slice.600
  70.6 1.5 constant_dynamic-slice_fusion.23
  72.1 4.9 multiply_convert_fusion.7
  77.0 1.3 slice.600
  78.9 58.0 %while.74 = (s32[]{:T(128)}, f32[2,64,512]{2,1,0:T(8,128)S(1)}, bf16[2,2,64,4096]{3,2,1,0:T(8,128)(2,1)}, f32[4,4096]{1,0:T(4,128)}, f32[2]{0:T(128)S(1)}, /*ind...) while((s32[]{:T(128)}, f32[2,64,512]{2,1,0:T(8,128)S(1)}, ...), condition=%wide.region_1.0_spmd.clone, body=%wide.region_0.0_spmd.clone.sunk | while | flops 138677248 | bytes 6719745 | solution.py:103
  79.9 4.4 multiply_convert_fusion.6
  84.3 1.3 slice.597
  87.2 4.4 multiply_convert_fusion.6
  91.6 1.3 slice.597
  94.4 4.4 multiply_convert_fusion.6
  98.8 1.3 slice.597
  101.7 4.4 multiply_convert_fusion.6
  108.9 4.4 multiply_convert_fusion.6
  113.3 1.3 slice.597
  116.2 4.4 multiply_convert_fusion.6
  123.4 4.4 multiply_convert_fusion.6
  130.7 4.4 multiply_convert_fusion.6
  139.7 157.6 %all-reduce.2.cloned.1.call-done = f32[2,2,64,512]{3,2,1,0:T(8,128)} async-done(((f32[2,2,64,512]{3,2,1,0:T(8,128)}), f32[2,2,64,512]{3,2,1,0:T(8,128)}) %all-reduce.2.cloned.1.call-update) | async-done | bytes 524304 | tf_op jit(solution)/shard_map/psum | solution.py:106
  299.5 1.6 broadcast.578.clone2
  301.1 59.4 %while.72 = (s32[]{:T(128)}, f32[128,4096]{1,0:T(8,128)}, f32[4,4096]{1,0:T(4,128)S(1)}, f32[4,4096]{1,0:T(4,128)S(1)}, f32[2]{0:T(128)S(1)}, /*index=5*/bf16[12...) while((s32[]{:T(128)}, f32[128,4096]{1,0:T(8,128)}, ...), condition=%wide.region_9.10_spmd.clone, body=%wide.region_5.9_spmd.clone.sunk | while | flops 275526656 | bytes 10699039 | solution.py:128
  301.9 5.1 multiply_reduce_fusion.6
  309.4 5.1 multiply_reduce_fusion.6
  316.8 5.1 multiply_reduce_fusion.6
  324.2 5.1 multiply_reduce_fusion.6
  331.6 5.1 multiply_reduce_fusion.6
  339.0 5.1 multiply_reduce_fusion.6
  346.4 5.1 multiply_reduce_fusion.6
  353.9 5.1 multiply_reduce_fusion.6
  360.5 1.6 broadcast.578.clone
  362.1 88.5 %while.73 = (s32[]{:T(128)}, f32[128,4096]{1,0:T(8,128)}, f32[4,4096]{1,0:T(4,128)S(1)}, f32[4,4096]{1,0:T(4,128)S(1)}, f32[2]{0:T(128)S(1)}, /*index=5*/bf16[12...) while((s32[]{:T(128)}, f32[128,4096]{1,0:T(8,128)}, ...), condition=%wide.region_14.15_spmd.clone, body=%wide.region_10.14_spmd.clone.sunk | while | flops 275526656 | bytes 10699047 | solution.py:128
  364.1 5.7 %multiply_reduce_fusion.7 = (f32[512]{0:T(512)S(1)}, f32[512]{0:T(512)S(1)}, f32[512]{0:T(512)S(1)}, bf16[512,512]{1,0:T(8,128)(2,1)S(1)}, bf16[512,512]{1,0:T(8,128)(2,1)S(1)}) fusion(f32[512]{0:T(512)S(1)} %bitcast.240, f32[512]{0:T(512)S(1)} %bitcast.246, f32[512]{0:T(512)S(1)} %neg.91, f32[512,1024]{1,0:T(8,128)S(1)} %fusion.121, ...), kind=kLoop, calls=%fused_computation.39.clone.1 | loop fusion | flops 4979200 | bytes 3164164 | tf_op jit(solution)/shard_map/while/body/eval_jaxpr/reduce_sum | solution.py:75
  375.1 5.7 %multiply_reduce_fusion.7 = (f32[512]{0:T(512)S(1)}, f32[512]{0:T(512)S(1)}, f32[512]{0:T(512)S(1)}, bf16[512,512]{1,0:T(8,128)(2,1)S(1)}, bf16[512,512]{1,0:T(8,128)(2,1)S(1)}) fusion(f32[512]{0:T(512)S(1)} %bitcast.240, f32[512]{0:T(512)S(1)} %bitcast.246, f32[512]{0:T(512)S(1)} %neg.91, f32[512,1024]{1,0:T(8,128)S(1)} %fusion.121, ...), kind=kLoop, calls=%fused_computation.39.clone.1 | loop fusion | flops 4979200 | bytes 3164164 | tf_op jit(solution)/shard_map/while/body/eval_jaxpr/reduce_sum | solution.py:75
  386.2 5.7 %multiply_reduce_fusion.7 = (f32[512]{0:T(512)S(1)}, f32[512]{0:T(512)S(1)}, f32[512]{0:T(512)S(1)}, bf16[512,512]{1,0:T(8,128)(2,1)S(1)}, bf16[512,512]{1,0:T(8,128)(2,1)S(1)}) fusion(f32[512]{0:T(512)S(1)} %bitcast.240, f32[512]{0:T(512)S(1)} %bitcast.246, f32[512]{0:T(512)S(1)} %neg.91, f32[512,1024]{1,0:T(8,128)S(1)} %fusion.121, ...), kind=kLoop, calls=%fused_computation.39.clone.1 | loop fusion | flops 4979200 | bytes 3164164 | tf_op jit(solution)/shard_map/while/body/eval_jaxpr/reduce_sum | solution.py:75
  397.2 5.7 %multiply_reduce_fusion.7 = (f32[512]{0:T(512)S(1)}, f32[512]{0:T(512)S(1)}, f32[512]{0:T(512)S(1)}, bf16[512,512]{1,0:T(8,128)(2,1)S(1)}, bf16[512,512]{1,0:T(8,128)(2,1)S(1)}) fusion(f32[512]{0:T(512)S(1)} %bitcast.240, f32[512]{0:T(512)S(1)} %bitcast.246, f32[512]{0:T(512)S(1)} %neg.91, f32[512,1024]{1,0:T(8,128)S(1)} %fusion.121, ...), kind=kLoop, calls=%fused_computation.39.clone.1 | loop fusion | flops 4979200 | bytes 3164164 | tf_op jit(solution)/shard_map/while/body/eval_jaxpr/reduce_sum | solution.py:75
  408.3 5.7 %multiply_reduce_fusion.7 = (f32[512]{0:T(512)S(1)}, f32[512]{0:T(512)S(1)}, f32[512]{0:T(512)S(1)}, bf16[512,512]{1,0:T(8,128)(2,1)S(1)}, bf16[512,512]{1,0:T(8,128)(2,1)S(1)}) fusion(f32[512]{0:T(512)S(1)} %bitcast.240, f32[512]{0:T(512)S(1)} %bitcast.246, f32[512]{0:T(512)S(1)} %neg.91, f32[512,1024]{1,0:T(8,128)S(1)} %fusion.121, ...), kind=kLoop, calls=%fused_computation.39.clone.1 | loop fusion | flops 4979200 | bytes 3164164 | tf_op jit(solution)/shard_map/while/body/eval_jaxpr/reduce_sum | solution.py:75
  419.4 5.7 %multiply_reduce_fusion.7 = (f32[512]{0:T(512)S(1)}, f32[512]{0:T(512)S(1)}, f32[512]{0:T(512)S(1)}, bf16[512,512]{1,0:T(8,128)(2,1)S(1)}, bf16[512,512]{1,0:T(8,128)(2,1)S(1)}) fusion(f32[512]{0:T(512)S(1)} %bitcast.240, f32[512]{0:T(512)S(1)} %bitcast.246, f32[512]{0:T(512)S(1)} %neg.91, f32[512,1024]{1,0:T(8,128)S(1)} %fusion.121, ...), kind=kLoop, calls=%fused_computation.39.clone.1 | loop fusion | flops 4979200 | bytes 3164164 | tf_op jit(solution)/shard_map/while/body/eval_jaxpr/reduce_sum | solution.py:75
  430.4 5.7 %multiply_reduce_fusion.7 = (f32[512]{0:T(512)S(1)}, f32[512]{0:T(512)S(1)}, f32[512]{0:T(512)S(1)}, bf16[512,512]{1,0:T(8,128)(2,1)S(1)}, bf16[512,512]{1,0:T(8,128)(2,1)S(1)}) fusion(f32[512]{0:T(512)S(1)} %bitcast.240, f32[512]{0:T(512)S(1)} %bitcast.246, f32[512]{0:T(512)S(1)} %neg.91, f32[512,1024]{1,0:T(8,128)S(1)} %fusion.121, ...), kind=kLoop, calls=%fused_computation.39.clone.1 | loop fusion | flops 4979200 | bytes 3164164 | tf_op jit(solution)/shard_map/while/body/eval_jaxpr/reduce_sum | solution.py:75
  441.5 5.7 %multiply_reduce_fusion.7 = (f32[512]{0:T(512)S(1)}, f32[512]{0:T(512)S(1)}, f32[512]{0:T(512)S(1)}, bf16[512,512]{1,0:T(8,128)(2,1)S(1)}, bf16[512,512]{1,0:T(8,128)(2,1)S(1)}) fusion(f32[512]{0:T(512)S(1)} %bitcast.240, f32[512]{0:T(512)S(1)} %bitcast.246, f32[512]{0:T(512)S(1)} %neg.91, f32[512,1024]{1,0:T(8,128)S(1)} %fusion.121, ...), kind=kLoop, calls=%fused_computation.39.clone.1 | loop fusion | flops 4979200 | bytes 3164164 | tf_op jit(solution)/shard_map/while/body/eval_jaxpr/reduce_sum | solution.py:75
  450.5 2.0 copy.11
  452.6 3.9 pad_maximum_fusion
  456.5 30.8 %reduce-scatter.7.cloned.1.call-done = f32[512,4]{1,0:T(8,128)} async-done(((f32[4096,4]{1,0:T(8,128)}), f32[512,4]{1,0:T(8,128)}) %reduce-scatter.7.cloned.1.call-update) | async-done | bytes 8208
  488.4 5.0 psum.15
  494.0 35.9 %reduce-scatter.5.cloned.1.call-done = f32[2,2,64,512]{3,2,1,0:T(8,128)} async-done(((f32[2,2,64,4096]{3,2,1,0:T(8,128)}), f32[2,2,64,512]{3,2,1,0:T(8,128)}) %reduce-scatter.5.cloned.1.call-update) | async-done | bytes 524304 | tf_op jit(solution)/shard_map/reduce_scatter | solution.py:134
  (364 shorter events, 93.3 us)
Async XLA Ops:
  7.2 290.2 %all-reduce.2.cloned.1.call-start = ((), (), s32[]{:S(2)}) async-start(), calls=%async_computation.2 | async-start | bytes 1048576 | tf_op jit(solution)/shard_map/psum | solution.py:106
  78.8 60.8 %copy-start.4 = (s32[64]{0:T(128)S(1)}, s32[64]{0:T(128)}, u32[]{:S(2)}) copy-start(s32[64]{0:T(128)} %param.17) | copy-start | bytes 772
  78.8 60.8 %copy-start.3 = (f32[2,64]{1,0:T(2,128)S(1)}, f32[2,64]{1,0:T(2,128)}, u32[]{:S(2)}) copy-start(f32[2,64]{1,0:T(2,128)} %param.15) | copy-start | bytes 1540
  137.7 163.5 %copy-start = (bf16[2,2,64,4096]{3,2,1,0:T(8,128)(2,1)S(1)}, bf16[2,2,64,4096]{3,2,1,0:T(8,128)(2,1)}, u32[]{:S(2)}) copy-start(bf16[2,2,64,4096]{3,2,1,0:T(8,128)(2,1)} %get-tuple-element.1416) | copy-start | bytes 6291460
  137.7 163.5 %copy-start.2 = (f32[4,4096]{1,0:T(4,128)S(1)}, f32[4,4096]{1,0:T(4,128)}, u32[]{:S(2)}) copy-start(f32[4,4096]{1,0:T(4,128)} %get-tuple-element.1429) | copy-start | bytes 196612
  137.7 349.6 %reduce-scatter.7.cloned.1.call-start = ((), (), s32[]{:S(2)}) async-start(), calls=%async_computation.4 | async-start | bytes 2359296
  450.5 2.1 copy-start.1
  452.5 77.4 %reduce-scatter.5.cloned.1.call-start = ((), (), s32[]{:S(2)}) async-start(), calls=%async_computation.3 | async-start | bytes 4718592 | tf_op jit(solution)/shard_map/reduce_scatter | solution.py:134
Sparse Core Ops, SparseCore 0:
  137.8 159.4 all-reduce.1
  452.7 34.6 reduce-scatter.6
  490.5 39.4 reduce-scatter.4
where the time goes:
time: 539 us; the launch traced here: 536 us
  waiting for transfers between devices  224 us (42%)
  other arithmetic  218 us (40%)
  local copies, waits for them, and re-layouts  52.7 us (10%)
  matrix products  19 us (4%)
  between operations  15.1 us (3%)
    psum x1, waiting for transfers between devices, body(): kochin = lax.psum(partial_kochin, 'panel')  158 us
    reduce_sum x16, other arithmetic, backward_block(): jnp.sum(twist * jnp.cos(angles)[None, :], 1)  85.8 us
    another operation x16, other arithmetic  74.2 us
    reduce_scatter x1, waiting for transfers between devices, body(): lax.psum_scatter(grads_all, 'dir', scatter_dimension=3, tiled=True)  35.9 us
    unnamed x4, waiting for transfers between devices  30.9 us
    slice x32, other arithmetic, phase_terms(): geometry[0][:, None] * jnp.cos(angles)[None, :]  26.9 us
    slice x16, local copies, waits for them, and re-layouts, add_block(): sig = lax.dynamic_slice_in_dim(sources[freq], start, block, 2)  20.7 us
    dynamic_update_slice x32, local copies, waits for them, and re-layouts, back_block(): grads_acc = lax.dynamic_update_slice_in_dim(grads_acc, dsig, start, 1)  14.1 us
  transfers between devices with their start and end apart: 3, of which 3 were waited for; matrix products, arithmetic and copies ran while one was open for 1% of the time, Pallas kernels for 0%

commit v1 on v0

--- a/solution.py
+++ b/solution.py
@@ -103,7 +103,7 @@
             lax.fori_loop(0, steps, add_block, jnp.zeros((2, heads, dir_count), jnp.float32))
         )
     partial_kochin = jnp.stack(kochin_parts)
-    kochin = lax.psum(partial_kochin, "panel")
+    kochin = jnp.sum(lax.all_gather(partial_kochin, "panel"), axis=0)
     cot = jnp.stack(
         [
             cotangent(kochin[freq], waves[freq], dir_ids, drift_cot[freq], heading_dir)

time: 539 us -> 520 us (0.965)
  waiting for transfers between devices: 224 us -> 201 us
    psum x1 -> x0, waiting for transfers between devices: 158 us -> none  [body(): kochin = lax.psum(partial_kochin, 'panel')]
    all_gather x0 -> x1, waiting for transfers between devices: none -> 135 us  [body(): kochin = jnp.sum(lax.all_gather(partial_kochin, 'panel'), axis=0)]
where the time goes in v1:
time: 520 us; the launch traced here: 518 us
  other arithmetic  222 us (43%)
  waiting for transfers between devices  201 us (39%)
  local copies, waits for them, and re-layouts  52.7 us (10%)
  matrix products  19.1 us (4%)
  between operations  15.1 us (3%)
    all_gather x1, waiting for transfers between devices, body(): kochin = jnp.sum(lax.all_gather(partial_kochin, 'panel'), axis=0)  135 us
    reduce_sum x16, other arithmetic, backward_block(): jnp.sum(twist * jnp.cos(angles)[None, :], 1)  85.8 us
    another operation x16, other arithmetic  74.9 us
    reduce_scatter x1, waiting for transfers between devices, body(): lax.psum_scatter(grads_all, 'dir', scatter_dimension=3, tiled=True)  35.9 us
    unnamed x4, waiting for transfers between devices  30.1 us
    slice x32, other arithmetic, phase_terms(): geometry[0][:, None] * jnp.cos(angles)[None, :]  27.5 us
    slice x16, local copies, waits for them, and re-layouts, add_block(): sig = lax.dynamic_slice_in_dim(sources[freq], start, block, 2)  20.7 us
    dynamic_update_slice x32, local copies, waits for them, and re-layouts, back_block(): grads_acc = lax.dynamic_update_slice_in_dim(grads_acc, dsig, start, 1)  14.1 us
  transfers between devices with their start and end apart: 3, of which 3 were waited for; matrix products, arithmetic and copies ran while one was open for 1% of the time, Pallas kernels for 0%

profile of v1, /device:TPU:8, one launch (start us, length us, event | category | flops | bytes accessed | tf_op | source)
XLA Modules:
  0.0 517.5 jit_solution(13872941885054928563)
XLA Ops:
  7.9 58.0 %while.74 = (s32[]{:T(128)}, f32[2,64,512]{2,1,0:T(8,128)S(1)}, bf16[2,2,64,4096]{3,2,1,0:T(8,128)(2,1)}, f32[4,4096]{1,0:T(4,128)}, f32[2]{0:T(128)S(1)}, /*ind...) while((s32[]{:T(128)}, f32[2,64,512]{2,1,0:T(8,128)S(1)}, ...), condition=%wide.region_1.0_spmd.clone, body=%wide.region_0.0_spmd.clone.sunk | while | flops 138677248 | bytes 6719737 | solution.py:103
  9.0 4.4 multiply_convert_fusion.6
  13.4 1.3 slice.597
  16.2 4.4 multiply_convert_fusion.6
  20.6 1.3 slice.597
  23.5 4.4 multiply_convert_fusion.6
  27.8 1.3 slice.597
  30.7 4.4 multiply_convert_fusion.6
  38.0 4.4 multiply_convert_fusion.6
  45.2 4.4 multiply_convert_fusion.6
  52.5 4.4 multiply_convert_fusion.6
  59.7 4.4 multiply_convert_fusion.6
  65.9 72.4 %while.75 = (s32[]{:T(128)}, f32[2,64,512]{2,1,0:T(8,128)S(1)}, bf16[2,2,64,4096]{3,2,1,0:T(8,128)(2,1)}, f32[4,4096]{1,0:T(4,128)}, f32[2]{0:T(128)S(1)}, /*ind...) while((s32[]{:T(128)}, f32[2,64,512]{2,1,0:T(8,128)S(1)}, ...), condition=%wide.region_3.0_spmd.clone, body=%wide.region_2.0_spmd.clone.sunk | while | flops 138677248 | bytes 6719745 | solution.py:103
  66.5 1.6 constant_dynamic-slice_fusion.23
  68.2 5.0 multiply_convert_fusion.7
  73.2 1.3 slice.600
  75.6 1.6 constant_dynamic-slice_fusion.23
  77.2 5.0 multiply_convert_fusion.7
  82.2 1.3 slice.600
  84.6 1.6 constant_dynamic-slice_fusion.23
  86.3 5.0 multiply_convert_fusion.7
  91.3 1.3 slice.600
  93.7 1.6 constant_dynamic-slice_fusion.23
  95.3 5.0 multiply_convert_fusion.7
  100.3 1.3 slice.600
  102.7 1.6 constant_dynamic-slice_fusion.23
  104.4 5.0 multiply_convert_fusion.7
  109.4 1.3 slice.600
  111.8 1.6 constant_dynamic-slice_fusion.23
  113.4 5.0 multiply_convert_fusion.7
  118.4 1.3 slice.600
  120.8 1.6 constant_dynamic-slice_fusion.23
  122.5 5.0 multiply_convert_fusion.7
  127.5 1.3 slice.600
  129.9 1.6 constant_dynamic-slice_fusion.23
  131.5 5.0 multiply_convert_fusion.7
  136.5 1.3 slice.600
  141.3 135.2 %all-gather.3.cloned.1.call-done = f32[32,2,64,512]{3,2,1,0:T(8,128)} async-done(((f32[2,2,64,512]{3,2,1,0:T(8,128)}), f32[32,2,64,512]{3,2,1,0:T(8,128)}) %all-gather.3.cloned.1.call-update) | async-done | bytes 8388624 | tf_op jit(solution)/shard_map/all_gather | solution.py:106
  276.5 4.4 reduce_sum.117
  281.2 1.6 broadcast.578.clone2
  282.8 59.4 %while.72 = (s32[]{:T(128)}, f32[128,4096]{1,0:T(8,128)}, f32[4,4096]{1,0:T(4,128)S(1)}, f32[4,4096]{1,0:T(4,128)S(1)}, f32[2]{0:T(128)S(1)}, /*index=5*/bf16[12...) while((s32[]{:T(128)}, f32[128,4096]{1,0:T(8,128)}, ...), condition=%wide.region_9.10_spmd.clone, body=%wide.region_5.9_spmd.clone.sunk | while | flops 275526656 | bytes 10699039 | solution.py:128
  283.6 5.1 multiply_reduce_fusion.6
  291.1 5.1 multiply_reduce_fusion.6
  298.5 5.1 multiply_reduce_fusion.6
  305.9 5.1 multiply_reduce_fusion.6
  313.3 5.1 multiply_reduce_fusion.6
  320.7 5.1 multiply_reduce_fusion.6
  328.2 5.1 multiply_reduce_fusion.6
  335.6 5.1 multiply_reduce_fusion.6
  342.3 1.6 broadcast.578.clone
  343.8 88.5 %while.73 = (s32[]{:T(128)}, f32[128,4096]{1,0:T(8,128)}, f32[4,4096]{1,0:T(4,128)S(1)}, f32[4,4096]{1,0:T(4,128)S(1)}, f32[2]{0:T(128)S(1)}, /*index=5*/bf16[12...) while((s32[]{:T(128)}, f32[128,4096]{1,0:T(8,128)}, ...), condition=%wide.region_14.15_spmd.clone, body=%wide.region_10.14_spmd.clone.sunk | while | flops 275526656 | bytes 10699047 | solution.py:128
  345.8 5.7 %multiply_reduce_fusion.7 = (f32[512]{0:T(512)S(1)}, f32[512]{0:T(512)S(1)}, f32[512]{0:T(512)S(1)}, bf16[512,512]{1,0:T(8,128)(2,1)S(1)}, bf16[512,512]{1,0:T(8,128)(2,1)S(1)}) fusion(f32[512]{0:T(512)S(1)} %bitcast.252, f32[512]{0:T(512)S(1)} %bitcast.244, f32[512]{0:T(512)S(1)} %neg.91, f32[512,1024]{1,0:T(8,128)S(1)} %fusion.121, ...), kind=kLoop, calls=%fused_computation.39.clone.1 | loop fusion | flops 4979200 | bytes 3164164 | tf_op jit(solution)/shard_map/while/body/eval_jaxpr/reduce_sum | solution.py:75
  356.9 5.7 %multiply_reduce_fusion.7 = (f32[512]{0:T(512)S(1)}, f32[512]{0:T(512)S(1)}, f32[512]{0:T(512)S(1)}, bf16[512,512]{1,0:T(8,128)(2,1)S(1)}, bf16[512,512]{1,0:T(8,128)(2,1)S(1)}) fusion(f32[512]{0:T(512)S(1)} %bitcast.252, f32[512]{0:T(512)S(1)} %bitcast.244, f32[512]{0:T(512)S(1)} %neg.91, f32[512,1024]{1,0:T(8,128)S(1)} %fusion.121, ...), kind=kLoop, calls=%fused_computation.39.clone.1 | loop fusion | flops 4979200 | bytes 3164164 | tf_op jit(solution)/shard_map/while/body/eval_jaxpr/reduce_sum | solution.py:75
  367.9 5.7 %multiply_reduce_fusion.7 = (f32[512]{0:T(512)S(1)}, f32[512]{0:T(512)S(1)}, f32[512]{0:T(512)S(1)}, bf16[512,512]{1,0:T(8,128)(2,1)S(1)}, bf16[512,512]{1,0:T(8,128)(2,1)S(1)}) fusion(f32[512]{0:T(512)S(1)} %bitcast.252, f32[512]{0:T(512)S(1)} %bitcast.244, f32[512]{0:T(512)S(1)} %neg.91, f32[512,1024]{1,0:T(8,128)S(1)} %fusion.121, ...), kind=kLoop, calls=%fused_computation.39.clone.1 | loop fusion | flops 4979200 | bytes 3164164 | tf_op jit(solution)/shard_map/while/body/eval_jaxpr/reduce_sum | solution.py:75
  379.0 5.7 %multiply_reduce_fusion.7 = (f32[512]{0:T(512)S(1)}, f32[512]{0:T(512)S(1)}, f32[512]{0:T(512)S(1)}, bf16[512,512]{1,0:T(8,128)(2,1)S(1)}, bf16[512,512]{1,0:T(8,128)(2,1)S(1)}) fusion(f32[512]{0:T(512)S(1)} %bitcast.252, f32[512]{0:T(512)S(1)} %bitcast.244, f32[512]{0:T(512)S(1)} %neg.91, f32[512,1024]{1,0:T(8,128)S(1)} %fusion.121, ...), kind=kLoop, calls=%fused_computation.39.clone.1 | loop fusion | flops 4979200 | bytes 3164164 | tf_op jit(solution)/shard_map/while/body/eval_jaxpr/reduce_sum | solution.py:75
  390.1 5.7 %multiply_reduce_fusion.7 = (f32[512]{0:T(512)S(1)}, f32[512]{0:T(512)S(1)}, f32[512]{0:T(512)S(1)}, bf16[512,512]{1,0:T(8,128)(2,1)S(1)}, bf16[512,512]{1,0:T(8,128)(2,1)S(1)}) fusion(f32[512]{0:T(512)S(1)} %bitcast.252, f32[512]{0:T(512)S(1)} %bitcast.244, f32[512]{0:T(512)S(1)} %neg.91, f32[512,1024]{1,0:T(8,128)S(1)} %fusion.121, ...), kind=kLoop, calls=%fused_computation.39.clone.1 | loop fusion | flops 4979200 | bytes 3164164 | tf_op jit(solution)/shard_map/while/body/eval_jaxpr/reduce_sum | solution.py:75
  401.1 5.7 %multiply_reduce_fusion.7 = (f32[512]{0:T(512)S(1)}, f32[512]{0:T(512)S(1)}, f32[512]{0:T(512)S(1)}, bf16[512,512]{1,0:T(8,128)(2,1)S(1)}, bf16[512,512]{1,0:T(8,128)(2,1)S(1)}) fusion(f32[512]{0:T(512)S(1)} %bitcast.252, f32[512]{0:T(512)S(1)} %bitcast.244, f32[512]{0:T(512)S(1)} %neg.91, f32[512,1024]{1,0:T(8,128)S(1)} %fusion.121, ...), kind=kLoop, calls=%fused_computation.39.clone.1 | loop fusion | flops 4979200 | bytes 3164164 | tf_op jit(solution)/shard_map/while/body/eval_jaxpr/reduce_sum | solution.py:75
  412.2 5.7 %multiply_reduce_fusion.7 = (f32[512]{0:T(512)S(1)}, f32[512]{0:T(512)S(1)}, f32[512]{0:T(512)S(1)}, bf16[512,512]{1,0:T(8,128)(2,1)S(1)}, bf16[512,512]{1,0:T(8,128)(2,1)S(1)}) fusion(f32[512]{0:T(512)S(1)} %bitcast.252, f32[512]{0:T(512)S(1)} %bitcast.244, f32[512]{0:T(512)S(1)} %neg.91, f32[512,1024]{1,0:T(8,128)S(1)} %fusion.121, ...), kind=kLoop, calls=%fused_computation.39.clone.1 | loop fusion | flops 4979200 | bytes 3164164 | tf_op jit(solution)/shard_map/while/body/eval_jaxpr/reduce_sum | solution.py:75
  423.2 5.7 %multiply_reduce_fusion.7 = (f32[512]{0:T(512)S(1)}, f32[512]{0:T(512)S(1)}, f32[512]{0:T(512)S(1)}, bf16[512,512]{1,0:T(8,128)(2,1)S(1)}, bf16[512,512]{1,0:T(8,128)(2,1)S(1)}) fusion(f32[512]{0:T(512)S(1)} %bitcast.252, f32[512]{0:T(512)S(1)} %bitcast.244, f32[512]{0:T(512)S(1)} %neg.91, f32[512,1024]{1,0:T(8,128)S(1)} %fusion.121, ...), kind=kLoop, calls=%fused_computation.39.clone.1 | loop fusion | flops 4979200 | bytes 3164164 | tf_op jit(solution)/shard_map/while/body/eval_jaxpr/reduce_sum | solution.py:75
  432.3 2.0 copy.11
  434.4 4.0 pad_maximum_fusion
  438.4 30.1 %reduce-scatter.7.cloned.1.call-done = f32[512,4]{1,0:T(8,128)} async-done(((f32[4096,4]{1,0:T(8,128)}), f32[512,4]{1,0:T(8,128)}) %reduce-scatter.7.cloned.1.call-update) | async-done | bytes 8208
  469.5 5.0 psum.7
  475.1 35.9 %reduce-scatter.5.cloned.1.call-done = f32[2,2,64,512]{3,2,1,0:T(8,128)} async-done(((f32[2,2,64,4096]{3,2,1,0:T(8,128)}), f32[2,2,64,512]{3,2,1,0:T(8,128)}) %reduce-scatter.5.cloned.1.call-update) | async-done | bytes 524304 | tf_op jit(solution)/shard_map/reduce_scatter | solution.py:134
  (365 shorter events, 92.7 us)
Async XLA Ops:
  7.2 269.3 %all-gather.3.cloned.1.call-start = ((), (), s32[]{:S(2)}) async-start(), calls=%async_computation.3 | async-start | bytes 8912896 | tf_op jit(solution)/shard_map/all_gather | solution.py:106
  65.9 75.3 %copy-start.4 = (s32[64]{0:T(128)S(1)}, s32[64]{0:T(128)}, u32[]{:S(2)}) copy-start(s32[64]{0:T(128)} %param.17) | copy-start | bytes 772
  65.9 75.4 %copy-start.3 = (f32[2,64]{1,0:T(2,128)S(1)}, f32[2,64]{1,0:T(2,128)}, u32[]{:S(2)}) copy-start(f32[2,64]{1,0:T(2,128)} %param.15) | copy-start | bytes 1540
  139.2 329.3 %reduce-scatter.7.cloned.1.call-start = ((), (), s32[]{:S(2)}) async-start(), calls=%async_computation.4 | async-start | bytes 2359296
  280.9 1.9 copy-start
  280.9 1.9 copy-start.2
  432.3 2.1 copy-start.1
  434.3 76.7 %reduce-scatter.5.cloned.1.call-start = ((), (), s32[]{:S(2)}) async-start(), calls=%async_computation.2 | async-start | bytes 4718592 | tf_op jit(solution)/shard_map/reduce_scatter | solution.py:134
Sparse Core Ops, SparseCore 0:
  139.3 137.1 all-gather.2
  434.4 34.0 reduce-scatter.6
  471.6 39.3 reduce-scatter.4
